TPU v7x, 32 devices: a whole 2x2x4 slice. The times are simulated.
32 devices in a mesh: rows: 8 (over z, x), chan: 4 (over y, core).
Axes of the slice: x: 2, y: 2, z: 4, core: 2. Of those that a mesh axis runs over, the one named last changes fastest.
Arguments:
- frames: bfloat16 [9, 32, 480, 256], P(None, 'rows', 'chan'), may hold values from -450 to 450
- spatial_weight: bfloat16 [256, 2304], P('rows'), may hold values from -0.125 to 0.125
- temporal_weight: bfloat16 [256, 768], P('rows'), may hold values from -0.21875 to 0.21875
- down_weight: bfloat16 [256, 2304], P('rows'), may hold values from -0.125 to 0.125
- norm_gain: float32 [256], replicated, may hold values from 0.5 to 1.5
- norm_shift: float32 [256], replicated, may hold values from -3 to 3
- down_bias: float32 [256], replicated, may hold values from -3 to 3
Outputs:
- latent: bfloat16 [9, 16, 240, 256], P(None, 'rows', 'chan')
All inputs are finite; a program needn't handle non-finite values.
Results may differ from a plain program's by a relative error of at most 0.0053.
Values may be sent and summed in bfloat16 or wider, within the bound.
No kernel may reach another device: no remote copies, remote signals or barrier semaphores. Data moves between devices by JAX's collectives and lax.ppermute only.
A program may use at most 128 MiB of HBM per device.

v0:
```python
import jax
import jax.numpy as jnp
from jax import lax
from jax.sharding import PartitionSpec as P

GROUPS = 32
epsilon = 1e-06


def extended_2(cells, sides, width):
    for axis, dim in sides:
        count = lax.axis_size(axis)
        ends = count - 1
        head = lax.slice_in_dim(cells, 0, width, axis=dim)
        tail = lax.slice_in_dim(cells, cells.shape[dim] - width, cells.shape[dim], axis=dim)
        cells = jnp.concatenate(
            [
                lax.ppermute(tail, axis, [(i, (i + 1) % count) for i in range(ends)]),
                cells,
                lax.ppermute(head, axis, [((i + 1) % count, i) for i in range(ends)]),
            ],
            axis=dim,
        )
    return cells


def passed_along(block, axis, distance):
    devices = range(lax.axis_size(axis))
    route = [(i - distance, i) for i in devices if i - distance in devices]
    return lax.ppermute(block, axis, route)


def spatial_taps(padded, weight_rows, width_out):
    rows_out = padded.shape[1] - 2
    cols_out = padded.shape[2] - 2
    summed = None
    for tap_index in range(9):
        row_offset = tap_index // 3
        col_offset = tap_index % 3
        window = padded[
            :, row_offset : row_offset + rows_out, col_offset : col_offset + cols_out, :
        ]
        weight_panel = weight_rows[:, tap_index * width_out : (tap_index + 1) * width_out]
        product = jnp.einsum(
            "fijc,co->fijo", window, weight_panel, preferred_element_type=jnp.float32
        )
        summed = product if summed is None else summed + product
    return summed


def temporal_taps(values, weight_rows, width_out):
    frame_count = values.shape[0]
    summed = None
    for tap_index in range(3):
        lag_frames = 2 - tap_index
        if lag_frames > 0:
            delayed = jnp.concatenate(
                [jnp.repeat(values[:1], lag_frames, axis=0), values[: frame_count - lag_frames]],
                axis=0,
            )
        else:
            delayed = values
        weight_panel = weight_rows[:, tap_index * width_out : (tap_index + 1) * width_out]
        product = jnp.einsum(
            "fijc,co->fijo", delayed, weight_panel, preferred_element_type=jnp.float32
        )
        summed = product if summed is None else summed + product
    return summed


def down_taps(extended, weight_rows, width_out):
    rows_out = (extended.shape[1] - 1) // 2
    cols_out = (extended.shape[2] - 1) // 2
    summed = None
    for tap_index in range(9):
        row_offset = tap_index // 3
        col_offset = tap_index % 3
        window = extended[
            :,
            row_offset : row_offset + 2 * rows_out : 2,
            col_offset : col_offset + 2 * cols_out : 2,
            :,
        ]
        weight_panel = weight_rows[:, tap_index * width_out : (tap_index + 1) * width_out]
        product = jnp.einsum(
            "fijc,co->fijo", window, weight_panel, preferred_element_type=jnp.float32
        )
        summed = product if summed is None else summed + product
    return summed


def group_reduce(partial_sums):
    return lax.psum(partial_sums, ("rows", "chan"))


def place_groups(channel_sums, group_width):
    local_sums = channel_sums.reshape(-1, group_width).sum(axis=1)
    return local_sums


def channel_values(group_vector, group_width):
    return jnp.repeat(group_vector, group_width)


def per_device(
    frames, spatial_weight, temporal_weight, down_weight, norm_gain, norm_shift, down_bias
):
    full_spatial, full_temporal, full_down = (
        lax.all_gather(spatial_weight, "rows", axis=0, tiled=True),
        lax.all_gather(temporal_weight, "rows", axis=0, tiled=True),
        lax.all_gather(down_weight, "rows", axis=0, tiled=True),
    )
    channels = full_spatial.shape[0]
    group_width = channels // GROUPS
    frame_count = frames.shape[0]
    rows_dev = frames.shape[1]
    width_all = frames.shape[2] * lax.axis_size("chan")
    cell_count = float(frame_count * rows_dev * lax.axis_size("rows") * width_all * group_width)
    padded = extended_2(frames, (("rows", 1), ("chan", 2)), 1)
    first = spatial_taps(padded, full_spatial, channels).astype(jnp.bfloat16)
    hidden = temporal_taps(first, full_temporal, channels)
    channel_sums = jnp.sum(hidden, axis=(0, 1, 2))
    totals = group_reduce(place_groups(channel_sums, group_width)[None])
    means = totals[0] / cell_count
    chan_mean = channel_values(means, group_width)
    centered = hidden - chan_mean
    spread = group_reduce(
        place_groups(jnp.sum(centered * centered, axis=(0, 1, 2)), group_width)[None]
    )
    variance = spread[0] / cell_count
    chan_var = channel_values(variance, group_width)
    act = jax.nn.silu(centered * lax.rsqrt(chan_var + epsilon) * norm_gain + norm_shift).astype(
        jnp.bfloat16
    )
    below = passed_along(act[:, :1], "rows", -1)
    extended = jnp.concatenate([act, below], axis=1)
    beside = passed_along(extended[:, :, :1], "chan", -1)
    extended = jnp.concatenate([extended, beside], axis=2)
    latent = down_taps(extended, full_down, channels) + down_bias
    return latent.astype(jnp.bfloat16)


def solution(mesh):
    placed = (
        P(None, "rows", "chan", None),
        P("rows", None),
        P("rows", None),
        P("rows", None),
        P(),
        P(),
        P(),
    )
    return jax.shard_map(
        per_device,
        mesh=mesh,
        in_specs=placed,
        out_specs=P(None, "rows", "chan", None),
        check_vma=False,
    )
```

profile of v0, /device:TPU:3, one launch (start us, length us, event | category | flops | bytes accessed | tf_op | source)
XLA Modules:
  0.0 319.5 jit_solution(4577024968184721207)
XLA Ops:
  7.3 2.1 fusion.64
  9.4 3.2 collective-permute-start
  12.6 2.9 collective-permute-start.1
  15.5 22.7 %collective-permute-done = bf16[9,1,120,256]{3,2,1,0:T(8,128)(2,1)} collective-permute-done((bf16[9,1,120,256]{3,2,1,0:T(8,128)(2,1)S(1)}, bf16[9,1,120,256]{3,2,1,0:T(8,128)(2,1)}, u32[]{:S(2)}, u32[]{:S(2)}) %collective-permute-start) | collective-permute-done | bytes 552992 | tf_op jit(solution)/shard_map/ppermute | solution.py:18
  42.3 4.6 %collective-permute-start.2 = (bf16[9,6,1,256]{3,2,1,0:T(2,128)(2,1)S(1)}, bf16[9,6,1,256]{3,2,1,0:T(2,128)(2,1)S(1)}, u32[]{:S(2)}, u32[]{:S(2)}) collective-permute-start(bf16[9,6,1,256]{3,2,1,0:T(2,128)(2,1)S(1)} %get-tuple-element.6), channel_id=1, source_target_pairs={{0,1},{1,2},{2,3},{4,5},{5,6},{6,7},{8,9},{9,10},{10,11},{12,13},{... | collective-permute-start | bytes 82952 | tf_op jit(solution)/shard_map/ppermute | solution.py:18
  46.9 25.9 %all_gather.10 = bf16[256,768]{1,0:T(8,128)(2,1)} all-gather(bf16[32,768]{1,0:T(8,128)(2,1)S(1)} %copy-done.12), channel_id=1, replica_groups=mesh['rows'=8,'chan'=4] {'rows'}, dimensions={0}, use_global_device_ids=true | all-gather | bytes 442368 | tf_op jit(solution)/shard_map/all_gather | solution.py:110
  72.8 5.5 %collective-permute-start.3 = (bf16[9,6,1,256]{3,2,1,0:T(2,128)(2,1)S(1)}, bf16[9,6,1,256]{3,2,1,0:T(2,128)(2,1)S(1)}, u32[]{:S(2)}, u32[]{:S(2)}) collective-permute-start(bf16[9,6,1,256]{3,2,1,0:T(2,128)(2,1)S(1)} %get-tuple-element.5), channel_id=1, source_target_pairs={{1,0},{2,1},{3,2},{5,4},{6,5},{7,6},{9,8},{10,9},{11,10},{13,12},{... | collective-permute-start | bytes 82952 | tf_op jit(solution)/shard_map/ppermute | solution.py:20
  78.4 3.8 %fusion.15 = f32[9,4,120,256]{3,2,1,0:T(8,128)} fusion(bf16[9,6,120,256]{3,2,1,0:T(8,128)(2,1)S(1)} %constant_dynamic-update-slice_fusion, bf16[9,6,1,256]{3,2,1,0:T(2,128)(2,1)S(1)} %collective-permute-done.2, bf16[256,2304]{1,0:T(8,128)(2,1)} %all-gather.3.cloned.1.call-done), kind=kOutput, calls=%fused_computation.29 | convolution fusion | flops 570654720 | bytes 7900160 | tf_op jit(solution)/shard_map/fijc,co->fijo/dot_general | solution.py:44
  82.2 2.9 fusion.18
  85.1 2.8 fusion.12
  87.8 2.9 fusion.9
  90.8 2.9 fusion.22
  93.6 3.9 %fusion = f32[9,4,120,256]{3,2,1,0:T(8,128)} fusion(bf16[9,4,120,256]{3,2,1,0:T(8,128)(2,1)S(1)} %copy-done, bf16[9,1,120,256]{3,2,1,0:T(8,128)(2,1)} %collective-permute-done, bf16[256,2304]{1,0:T(8,128)(2,1)S(1)} %copy-done.11), kind=kOutput, calls=%fused_computation.15 | convolution fusion | flops 571760640 | bytes 7319552 | tf_op jit(solution)/shard_map/fijc,co->fijo/dot_general | solution.py:44
  99.3 2.9 fusion.50
  102.2 12.6 %add_convert_fusion = bf16[9,4,120,256]{3,2,1,0:T(8,128)(2,1)} fusion(f32[9,4,120,256]{3,2,1,0:T(8,128)S(1)} %fusion.4, f32[9,4,120,256]{3,2,1,0:T(8,128)} %fusion.22, f32[9,4,120,256]{3,2,1,0:T(8,128)} %fusion.9, f32[9,4,120,256]{3,2,1,0:T(8,128)} %fusion.50, f32[9,4,120,256]{3,2,1,0:T(8,128)} %fusion.15, f32[9,4,120,256]{3,2,1,0:T(8,128)} %fusion.12, ...), kind=kOutput, calls=%fused_computation.7 | convolution fusion | flops 580608000 | bytes 41105408 | tf_op jit(solution)/shard_map/fijc,co->fijo/dot_general | solution.py:44
  120.4 3.0 fusion.65
  123.7 38.6 %psum.14 = f32[1,32]{1,0:T(1,128)S(1)} all-reduce(f32[1,32]{1,0:T(1,128)S(1)} %bitcast.127), channel_id=1, replica_groups=mesh['rows'=8,'chan'=4] {'rows','chan'}, use_global_device_ids=true, to_apply=%region_2.0 | all-reduce | flops 32 | bytes 256 | tf_op jit(solution)/shard_map/psum | solution.py:93
  162.5 2.9 multiply_reduce_fusion
  165.5 41.8 %psum.15 = f32[1,32]{1,0:T(1,128)S(1)} all-reduce(f32[1,32]{1,0:T(1,128)S(1)} %bitcast.126), channel_id=1, replica_groups=mesh['rows'=8,'chan'=4] {'rows','chan'}, use_global_device_ids=true, to_apply=%region_5.0 | all-reduce | flops 32 | bytes 256 | tf_op jit(solution)/shard_map/psum | solution.py:93
  207.5 3.6 %multiply_convert_fusion = bf16[9,4,120,256]{3,2,1,0:T(8,128)(2,1)S(1)} fusion(f32[9,4,120,256]{3,2,1,0:T(8,128)} %get-tuple-element.12, f32[256]{0:T(256)S(1)} %copy-done.13, f32[256]{0:T(256)S(1)} %copy-done.14, f32[256]{0:T(256)S(1)} %rsqrt.16, f32[256]{0:T(256)S(1)} %sub.10), kind=kLoop, calls=%fused_computation.4 | loop fusion | flops 9953280 | bytes 6639616 | tf_op jit(solution)/shard_map/convert_element_type | solution.py:132
  214.8 2.2 fusion.48
  217.1 10.4 %collective-permute-done.4 = bf16[9,1,120,256]{3,2,1,0:T(8,128)(2,1)S(1)} collective-permute-done((bf16[9,1,120,256]{3,2,1,0:T(8,128)(2,1)}, bf16[9,1,120,256]{3,2,1,0:T(8,128)(2,1)S(1)}, u32[]{:S(2)}, u32[]{:S(2)}) %collective-permute-start.4) | collective-permute-done | bytes 552992 | tf_op jit(solution)/shard_map/ppermute | solution.py:30
  229.3 10.3 %slice.188 = bf16[9,2,60,256]{3,2,1,0:T(8,128)(2,1)} slice(bf16[9,5,120,256]{3,2,1,0:T(8,128)(2,1)} %pad_maximum_fusion), slice={[0:9:1], [1:5:2], [0:120:2], [0:256:1]} | slice | bytes 1105920 | tf_op jit(solution)/shard_map/slice | solution.py:78
  239.6 8.5 %slice.194 = bf16[9,2,60,256]{3,2,1,0:T(8,128)(2,1)S(1)} slice(bf16[9,5,120,256]{3,2,1,0:T(8,128)(2,1)} %pad_maximum_fusion), slice={[0:9:1], [2:5:2], [0:120:2], [0:256:1]} | slice | bytes 1105920 | tf_op jit(solution)/shard_map/slice | solution.py:78
  248.2 4.5 %collective-permute-start.5 = (bf16[9,5,1,256]{3,2,1,0:T(2,128)(2,1)S(1)}, bf16[9,5,1,256]{3,2,1,0:T(2,128)(2,1)S(1)}, u32[]{:S(2)}, u32[]{:S(2)}) collective-permute-start(bf16[9,5,1,256]{3,2,1,0:T(2,128)(2,1)S(1)} %fusion.51), channel_id=1, source_target_pairs={{1,0},{2,1},{3,2},{5,4},{6,5},{7,6},{9,8},{10,9},{11,10},{13,12},{... | collective-permute-start | bytes 69128 | tf_op jit(solution)/shard_map/ppermute | solution.py:30
  252.7 2.3 fusion.47
  254.9 2.2 fusion.44
  259.2 10.5 %slice.184 = bf16[9,2,60,256]{3,2,1,0:T(8,128)(2,1)} slice(bf16[9,5,121,256]{3,2,1,0:T(8,128)(2,1)} %pad_maximum_fusion.1), slice={[0:9:1], [0:4:2], [1:121:2], [0:256:1]} | slice | bytes 1105920 | tf_op jit(solution)/shard_map/slice | solution.py:78
  269.6 10.2 %slice.198 = bf16[9,2,60,256]{3,2,1,0:T(8,128)(2,1)} slice(bf16[9,5,121,256]{3,2,1,0:T(8,128)(2,1)} %pad_maximum_fusion.1), slice={[0:9:1], [2:5:2], [2:121:2], [0:256:1]} | slice | bytes 1105920 | tf_op jit(solution)/shard_map/slice | solution.py:78
  279.8 10.1 %slice.196 = bf16[9,2,60,256]{3,2,1,0:T(8,128)(2,1)} slice(bf16[9,5,121,256]{3,2,1,0:T(8,128)(2,1)} %pad_maximum_fusion.1), slice={[0:9:1], [2:5:2], [1:121:2], [0:256:1]} | slice | bytes 1105920 | tf_op jit(solution)/shard_map/slice | solution.py:78
  289.9 6.0 %slice.192 = bf16[9,2,60,256]{3,2,1,0:T(8,128)(2,1)} slice(bf16[9,5,121,256]{3,2,1,0:T(8,128)(2,1)S(1)} %copy-done.2), slice={[0:9:1], [1:5:2], [2:121:2], [0:256:1]} | slice | bytes 1105920 | tf_op jit(solution)/shard_map/slice | solution.py:78
  295.9 5.9 %slice.190 = bf16[9,2,60,256]{3,2,1,0:T(8,128)(2,1)} slice(bf16[9,5,121,256]{3,2,1,0:T(8,128)(2,1)S(1)} %copy-done.2), slice={[0:9:1], [1:5:2], [1:121:2], [0:256:1]} | slice | bytes 1105920 | tf_op jit(solution)/shard_map/slice | solution.py:78
  (79 shorter events, 31.2 us)
Async XLA Ops:
  6.5 71.8 %all-gather.3.cloned.1.call-start = ((), (), s32[]{:S(2)}) async-start(), calls=%async_computation | async-start | bytes 1327104 | tf_op jit(solution)/shard_map/all_gather | solution.py:109
  7.3 207.6 %all-gather.5.cloned.1.call-start = ((), (), s32[]{:S(2)}) async-start(), calls=%async_computation.1 | async-start | bytes 1327104 | tf_op jit(solution)/shard_map/all_gather | solution.py:111
  9.4 28.8 %collective-permute-start = (bf16[9,1,120,256]{3,2,1,0:T(8,128)(2,1)S(1)}, bf16[9,1,120,256]{3,2,1,0:T(8,128)(2,1)}, u32[]{:S(2)}, u32[]{:S(2)}) collective-permute-start(bf16[9,1,120,256]{3,2,1,0:T(8,128)(2,1)S(1)} %get-tuple-element.9), channel_id=1, source_target_pairs={{0,4},{4,8},{8,12},{12,16},{16,20},{20,24},{24,28},{1,5},{5,9},{9,... | collective-permute-start | bytes 1658888 | tf_op jit(solution)/shard_map/ppermute | solution.py:18
  12.6 28.5 %collective-permute-start.1 = (bf16[9,1,120,256]{3,2,1,0:T(8,128)(2,1)}, bf16[9,1,120,256]{3,2,1,0:T(8,128)(2,1)}, u32[]{:S(2)}, u32[]{:S(2)}) collective-permute-start(bf16[9,1,120,256]{3,2,1,0:T(8,128)(2,1)} %get-tuple-element.10), channel_id=1, source_target_pairs={{4,0},{8,4},{12,8},{16,12},{20,16},{24,20},{28,24},{5,1},{9,5},{13... | collective-permute-start | bytes 1658888 | tf_op jit(solution)/shard_map/ppermute | solution.py:20
  39.3 7.6 %copy-start.12 = (bf16[32,768]{1,0:T(8,128)(2,1)S(1)}, bf16[32,768]{1,0:T(8,128)(2,1)}, u32[]{:S(2)}) copy-start(bf16[32,768]{1,0:T(8,128)(2,1)} %param.9) | copy-start | bytes 147460
  42.3 36.0 %collective-permute-start.2 = (bf16[9,6,1,256]{3,2,1,0:T(2,128)(2,1)S(1)}, bf16[9,6,1,256]{3,2,1,0:T(2,128)(2,1)S(1)}, u32[]{:S(2)}, u32[]{:S(2)}) collective-permute-start(bf16[9,6,1,256]{3,2,1,0:T(2,128)(2,1)S(1)} %get-tuple-element.6), channel_id=1, source_target_pairs={{0,1},{1,2},{2,3},{4,5},{5,6},{6,7},{8,9},{9,10},{10,11},{12,13},{... | collective-permute-start | bytes 82952 | tf_op jit(solution)/shard_map/ppermute | solution.py:18
  72.8 12.3 %collective-permute-start.3 = (bf16[9,6,1,256]{3,2,1,0:T(2,128)(2,1)S(1)}, bf16[9,6,1,256]{3,2,1,0:T(2,128)(2,1)S(1)}, u32[]{:S(2)}, u32[]{:S(2)}) collective-permute-start(bf16[9,6,1,256]{3,2,1,0:T(2,128)(2,1)S(1)} %get-tuple-element.5), channel_id=1, source_target_pairs={{1,0},{2,1},{3,2},{5,4},{6,5},{7,6},{9,8},{10,9},{11,10},{13,12},{... | collective-permute-start | bytes 82952 | tf_op jit(solution)/shard_map/ppermute | solution.py:20
  78.4 3.8 %copy-start.11 = (bf16[256,2304]{1,0:T(8,128)(2,1)S(1)}, bf16[256,2304]{1,0:T(8,128)(2,1)}, u32[]{:S(2)}) copy-start(bf16[256,2304]{1,0:T(8,128)(2,1)} %all-gather.3.cloned.1.call-done) | copy-start | bytes 3538948
  90.8 2.9 copy-start
  114.8 1.6 copy-start.1
  116.4 1.0 copy-start.10
  117.4 1.5 slice-start
  118.9 1.5 slice-start.1
  123.5 84.1 %copy-start.13 = (f32[256]{0:T(256)S(1)}, f32[256]{0:T(256)}, u32[]{:S(2)}) copy-start(f32[256]{0:T(256)} %param.12) | copy-start | bytes 3076
  123.5 84.1 %copy-start.14 = (f32[256]{0:T(256)S(1)}, f32[256]{0:T(256)}, u32[]{:S(2)}) copy-start(f32[256]{0:T(256)} %param.11) | copy-start | bytes 3076
  212.0 15.5 %collective-permute-start.4 = (bf16[9,1,120,256]{3,2,1,0:T(8,128)(2,1)}, bf16[9,1,120,256]{3,2,1,0:T(8,128)(2,1)S(1)}, u32[]{:S(2)}, u32[]{:S(2)}) collective-permute-start(bf16[9,1,120,256]{3,2,1,0:T(8,128)(2,1)} %slice.226), channel_id=1, source_target_pairs={{4,0},{8,4},{12,8},{16,12},{20,16},{24,20},{28,24},{5,1},{9,5},{13... | collective-permute-start | bytes 1658888 | tf_op jit(solution)/shard_map/ppermute | solution.py:30
  248.1 4.6 %copy-start.8 = (bf16[9,2,60,256]{3,2,1,0:T(8,128)(2,1)S(1)}, bf16[9,2,60,256]{3,2,1,0:T(8,128)(2,1)}, u32[]{:S(2)}) copy-start(bf16[9,2,60,256]{3,2,1,0:T(8,128)(2,1)} %slice.188) | copy-start | bytes 1658884
  248.2 9.0 %collective-permute-start.5 = (bf16[9,5,1,256]{3,2,1,0:T(2,128)(2,1)S(1)}, bf16[9,5,1,256]{3,2,1,0:T(2,128)(2,1)S(1)}, u32[]{:S(2)}, u32[]{:S(2)}) collective-permute-start(bf16[9,5,1,256]{3,2,1,0:T(2,128)(2,1)S(1)} %fusion.51), channel_id=1, source_target_pairs={{1,0},{2,1},{3,2},{5,4},{6,5},{7,6},{9,8},{10,9},{11,10},{13,12},{... | collective-permute-start | bytes 69128 | tf_op jit(solution)/shard_map/ppermute | solution.py:30
  259.2 30.7 %copy-start.2 = (bf16[9,5,121,256]{3,2,1,0:T(8,128)(2,1)S(1)}, bf16[9,5,121,256]{3,2,1,0:T(8,128)(2,1)}, u32[]{:S(2)}) copy-start(bf16[9,5,121,256]{3,2,1,0:T(8,128)(2,1)} %pad_maximum_fusion.1) | copy-start | bytes 8363524
  302.8 3.1 copy-start.9
  302.8 4.3 %copy-start.7 = (bf16[9,2,60,256]{3,2,1,0:T(8,128)(2,1)S(1)}, bf16[9,2,60,256]{3,2,1,0:T(8,128)(2,1)}, u32[]{:S(2)}) copy-start(bf16[9,2,60,256]{3,2,1,0:T(8,128)(2,1)} %slice.190) | copy-start | bytes 1658884
  304.3 4.2 %copy-start.5 = (f32[9,2,60,256]{3,2,1,0:T(8,128)S(1)}, f32[9,2,60,256]{3,2,1,0:T(8,128)}, u32[]{:S(2)}) copy-start(f32[9,2,60,256]{3,2,1,0:T(8,128)} %fusion.48) | copy-start | bytes 3317764
  304.3 4.2 %copy-start.6 = (bf16[9,2,60,256]{3,2,1,0:T(8,128)(2,1)S(1)}, bf16[9,2,60,256]{3,2,1,0:T(8,128)(2,1)}, u32[]{:S(2)}) copy-start(bf16[9,2,60,256]{3,2,1,0:T(8,128)(2,1)} %slice.184) | copy-start | bytes 1658884
  307.1 2.6 copy-start.3
  307.1 2.6 copy-start.4
  307.1 2.6 copy-start.15
Sparse Core Ops, SparseCore 0:
  9.5 52.3 all-gather.2
  64.2 39.7 all-gather.4
where the time goes:
time: 322 us; the launch traced here: 320 us
  blocking collectives  106 us (33%)
  local copies, waits for them, and re-layouts  76.4 us (24%)
  matrix products  56 us (17%)
  waiting for transfers between devices  33.9 us (11%)
  starting transfers between devices  22.6 us (7%)
  between operations  13.8 us (4%)
  other arithmetic  10.5 us (3%)
    psum x2, blocking collectives, group_reduce(): return lax.psum(partial_sums, ('rows', 'chan'))  80.4 us
    slice x9, local copies, waits for them, and re-layouts, down_taps(): extended[:, row_offset:row_offset + 2 * rows_out:2, col_offset:col_offset...  63.3 us
    dot_general x9, matrix products, spatial_taps(): jnp.einsum('fijc,co->fijo', window, weight_panel, preferred_element_type=...  36.4 us
    all_gather x1, blocking collectives, per_device(): lax.all_gather(temporal_weight, 'rows', axis=0, tiled=True)  25.9 us
    ppermute x2, waiting for transfers between devices, extended_2(): lax.ppermute(tail, axis, [(i, (i + 1) % count) for i in range(ends)])  22.7 us
    dot_general x9, matrix products, down_taps(): jnp.einsum('fijc,co->fijo', window, weight_panel, preferred_element_type=...  15.1 us
    ppermute x2, waiting for transfers between devices, passed_along(): return lax.ppermute(block, axis, route)  10.4 us
    ppermute x2, starting transfers between devices, extended_2(): lax.ppermute(head, axis, [((i + 1) % count, i) for i in range(ends)])  8.43 us
  transfers between devices with their start and end apart: 8, of which 2 were waited for; matrix products, arithmetic and copies ran while one was open for 20% of the time, Pallas kernels for 0%

commit v1 on v0

--- a/solution.py
+++ b/solution.py
@@ -5,6 +5,27 @@
 
 GROUPS = 32
 epsilon = 1e-06
+
+
+def collect(x, axis, dim):
+    size, position, width = (lax.axis_size(axis), lax.axis_index(axis), x.shape[dim])
+    upward = [(i, (i + 1) % size) for i in range(size)]
+    downward = [(i, (i - 1) % size) for i in range(size)]
+    out = jnp.zeros((*x.shape[:dim], size * width, *x.shape[dim + 1 :]), x.dtype)
+    out = lax.dynamic_update_slice_in_dim(out, x, position * width, axis=dim)
+    from_left = from_right = x
+    half = size // 2
+    for hop in range(1, half + 1):
+        from_left = lax.ppermute(from_left, axis, upward)
+        out = lax.dynamic_update_slice_in_dim(
+            out, from_left, (position - hop) % size * width, axis=dim
+        )
+        if hop < size - half:
+            from_right = lax.ppermute(from_right, axis, downward)
+            out = lax.dynamic_update_slice_in_dim(
+                out, from_right, (position + hop) % size * width, axis=dim
+            )
+    return out
 
 
 def extended_2(cells, sides, width):
@@ -107,7 +128,7 @@
 ):
     full_spatial, full_temporal, full_down = (
         lax.all_gather(spatial_weight, "rows", axis=0, tiled=True),
-        lax.all_gather(temporal_weight, "rows", axis=0, tiled=True),
+        collect(temporal_weight, "rows", 0),
         lax.all_gather(down_weight, "rows", axis=0, tiled=True),
     )
     channels = full_spatial.shape[0]

time: 322 us -> 310 us (0.963)
  blocking collectives: 106 us -> 81.9 us
  starting transfers between devices: 22.6 us -> 29.6 us
  waiting for transfers between devices: 33.9 us -> 37.4 us
    ppermute x0 -> x7, waiting for transfers between devices: none -> 28.4 us  [the longest x4 28.3 us: collect(): from_left = lax.ppermute(from_left, axis, upward)]
    all_gather x1 -> x0, blocking collectives: 25.9 us -> none  [per_device(): lax.all_gather(temporal_weight, 'rows', axis=0, tiled=True)]
    ppermute x2, waiting for transfers between devices: 22.7 us -> 0.01 us  [extended_2(): lax.ppermute(tail, axis, [(i, (i + 1) % count) for i in range(ends)])]
    ppermute x0 -> x7, starting transfers between devices: none -> 6.47 us  [the longest x3 3.31 us: collect(): from_right = lax.ppermute(from_right, axis, downward)]
  transfers between devices with their start and end apart: 8 -> 15, of which waited for: 2 -> 5; matrix products, arithmetic and copies ran while one was open for 20% -> 21% of each run, Pallas kernels for 0% -> 0%
where the time goes in v1:
time: 310 us; the launch traced here: 308 us
  blocking collectives  81.9 us (26%)
  local copies, waits for them, and re-layouts  77.3 us (25%)
  matrix products  56.9 us (18%)
  waiting for transfers between devices  37.4 us (12%)
  starting transfers between devices  29.6 us (10%)
  between operations  14 us (5%)
  other arithmetic  10.5 us (3%)
    psum x2, blocking collectives, group_reduce(): return lax.psum(partial_sums, ('rows', 'chan'))  81.9 us
    slice x9, local copies, waits for them, and re-layouts, down_taps(): extended[:, row_offset:row_offset + 2 * rows_out:2, col_offset:col_offset...  62.8 us
    dot_general x9, matrix products, spatial_taps(): jnp.einsum('fijc,co->fijo', window, weight_panel, preferred_element_type=...  37.3 us
    ppermute x4, waiting for transfers between devices, collect(): from_left = lax.ppermute(from_left, axis, upward)  28.3 us
    dot_general x9, matrix products, down_taps(): jnp.einsum('fijc,co->fijo', window, weight_panel, preferred_element_type=...  15.1 us
    ppermute x2, starting transfers between devices, passed_along(): return lax.ppermute(block, axis, route)  8.57 us
    ppermute x2, waiting for transfers between devices, passed_along(): return lax.ppermute(block, axis, route)  8.26 us
    ppermute x2, starting transfers between devices, extended_2(): lax.ppermute(tail, axis, [(i, (i + 1) % count) for i in range(ends)])  7.6 us
  transfers between devices with their start and end apart: 15, of which 5 were waited for; matrix products, arithmetic and copies ran while one was open for 21% of the time, Pallas kernels for 0%

profile of v1, /device:TPU:3, one launch (start us, length us, event | category | flops | bytes accessed | tf_op | source)
XLA Modules:
  0.0 307.6 jit_solution(16994905948190620888)
XLA Ops:
  8.8 2.1 fusion.62
  10.9 5.0 %collective-permute-start.1 = (bf16[9,1,120,256]{3,2,1,0:T(8,128)(2,1)}, bf16[9,1,120,256]{3,2,1,0:T(8,128)(2,1)}, u32[]{:S(2)}, u32[]{:S(2)}) collective-permute-start(bf16[9,1,120,256]{3,2,1,0:T(8,128)(2,1)} %get-tuple-element.10), channel_id=1, source_target_pairs={{4,0},{8,4},{12,8},{16,12},{20,16},{24,20},{28,24},{5,1},{9,5},{13... | collective-permute-start | bytes 1658888 | tf_op jit(solution)/shard_map/ppermute | solution.py:41
  20.5 23.5 %collective-permute-done.6 = bf16[32,768]{1,0:T(8,128)(2,1)S(1)} collective-permute-done((bf16[32,768]{1,0:T(8,128)(2,1)S(1)}, bf16[32,768]{1,0:T(8,128)(2,1)S(1)}, u32[]{:S(2)}, u32[]{:S(2)}) %collective-permute-start.6) | collective-permute-done | bytes 49184 | tf_op jit(solution)/shard_map/ppermute | solution.py:19
  48.1 3.3 %collective-permute-done.10 = bf16[32,768]{1,0:T(8,128)(2,1)S(1)} collective-permute-done((bf16[32,768]{1,0:T(8,128)(2,1)S(1)}, bf16[32,768]{1,0:T(8,128)(2,1)S(1)}, u32[]{:S(2)}, u32[]{:S(2)}) %collective-permute-start.10) | collective-permute-done | bytes 49184 | tf_op jit(solution)/shard_map/ppermute | solution.py:19
  56.3 5.7 %collective-permute-start.2 = (bf16[9,6,1,256]{3,2,1,0:T(2,128)(2,1)S(1)}, bf16[9,6,1,256]{3,2,1,0:T(2,128)(2,1)S(1)}, u32[]{:S(2)}, u32[]{:S(2)}) collective-permute-start(bf16[9,6,1,256]{3,2,1,0:T(2,128)(2,1)S(1)} %get-tuple-element.6), channel_id=1, source_target_pairs={{0,1},{1,2},{2,3},{4,5},{5,6},{6,7},{8,9},{9,10},{10,11},{12,13},{... | collective-permute-start | bytes 82952 | tf_op jit(solution)/shard_map/ppermute | solution.py:39
  64.0 4.6 %fusion.48 = f32[9,4,120,256]{3,2,1,0:T(8,128)} fusion(bf16[9,4,120,256]{3,2,1,0:T(8,128)(2,1)} %param.7, bf16[256,2304]{1,0:T(8,128)(2,1)} %all-gather.3.cloned.1.call-done), kind=kOutput, calls=%fused_computation.81 | convolution fusion | flops 566231040 | bytes 6766592 | tf_op jit(solution)/shard_map/fijc,co->fijo/dot_general | solution.py:65
  70.4 2.8 fusion.22
  73.2 2.8 fusion.15
  76.0 2.9 fusion.9
  78.9 2.9 fusion.12
  81.8 2.9 fusion.18
  84.6 3.9 %fusion = f32[9,4,120,256]{3,2,1,0:T(8,128)} fusion(bf16[9,4,120,256]{3,2,1,0:T(8,128)(2,1)S(1)} %copy-done, bf16[9,1,120,256]{3,2,1,0:T(8,128)(2,1)} %collective-permute-done, bf16[256,2304]{1,0:T(8,128)(2,1)S(1)} %copy-done.13), kind=kOutput, calls=%fused_computation.15 | convolution fusion | flops 571760640 | bytes 7319552 | tf_op jit(solution)/shard_map/fijc,co->fijo/dot_general | solution.py:65
  88.6 12.8 %add_convert_fusion = bf16[9,4,120,256]{3,2,1,0:T(8,128)(2,1)} fusion(f32[9,4,120,256]{3,2,1,0:T(8,128)S(1)} %fusion.4, f32[9,4,120,256]{3,2,1,0:T(8,128)} %fusion.22, f32[9,4,120,256]{3,2,1,0:T(8,128)} %fusion.9, f32[9,4,120,256]{3,2,1,0:T(8,128)} %fusion.48, f32[9,4,120,256]{3,2,1,0:T(8,128)} %fusion.15, f32[9,4,120,256]{3,2,1,0:T(8,128)} %fusion.12, ...), kind=kOutput, calls=%fused_computation.7 | convolution fusion | flops 580608000 | bytes 41105408 | tf_op jit(solution)/shard_map/fijc,co->fijo/dot_general | solution.py:65
  107.6 3.0 fusion.63
  110.8 41.2 %psum.14 = f32[1,32]{1,0:T(1,128)S(1)} all-reduce(f32[1,32]{1,0:T(1,128)S(1)} %bitcast.129), channel_id=1, replica_groups=mesh['rows'=8,'chan'=4] {'rows','chan'}, use_global_device_ids=true, to_apply=%region_2.3 | all-reduce | flops 32 | bytes 256 | tf_op jit(solution)/shard_map/psum | solution.py:114
  152.2 2.9 multiply_reduce_fusion
  155.3 40.7 %psum.15 = f32[1,32]{1,0:T(1,128)S(1)} all-reduce(f32[1,32]{1,0:T(1,128)S(1)} %bitcast.128), channel_id=1, replica_groups=mesh['rows'=8,'chan'=4] {'rows','chan'}, use_global_device_ids=true, to_apply=%region_5.6 | all-reduce | flops 32 | bytes 256 | tf_op jit(solution)/shard_map/psum | solution.py:114
  196.1 3.6 %multiply_convert_fusion = bf16[9,4,120,256]{3,2,1,0:T(8,128)(2,1)S(1)} fusion(f32[9,4,120,256]{3,2,1,0:T(8,128)} %get-tuple-element.12, f32[256]{0:T(256)S(1)} %copy-done.15, f32[256]{0:T(256)S(1)} %copy-done.16, f32[256]{0:T(256)S(1)} %rsqrt.16, f32[256]{0:T(256)S(1)} %sub.26), kind=kLoop, calls=%fused_computation.4 | loop fusion | flops 9953280 | bytes 6639616 | tf_op jit(solution)/shard_map/convert_element_type | solution.py:153
  200.6 2.7 collective-permute-start.11
  204.3 2.2 fusion.46
  206.5 8.3 %collective-permute-done.11 = bf16[9,1,120,256]{3,2,1,0:T(8,128)(2,1)S(1)} collective-permute-done((bf16[9,1,120,256]{3,2,1,0:T(8,128)(2,1)}, bf16[9,1,120,256]{3,2,1,0:T(8,128)(2,1)S(1)}, u32[]{:S(2)}, u32[]{:S(2)}) %collective-permute-start.11) | collective-permute-done | bytes 552992 | tf_op jit(solution)/shard_map/ppermute | solution.py:51
  216.5 10.0 %slice.194 = bf16[9,2,60,256]{3,2,1,0:T(8,128)(2,1)} slice(bf16[9,5,120,256]{3,2,1,0:T(8,128)(2,1)} %pad_maximum_fusion), slice={[0:9:1], [2:5:2], [0:120:2], [0:256:1]} | slice | bytes 1105920 | tf_op jit(solution)/shard_map/slice | solution.py:99
  226.5 8.6 %slice.188 = bf16[9,2,60,256]{3,2,1,0:T(8,128)(2,1)S(1)} slice(bf16[9,5,120,256]{3,2,1,0:T(8,128)(2,1)} %pad_maximum_fusion), slice={[0:9:1], [1:5:2], [0:120:2], [0:256:1]} | slice | bytes 1105920 | tf_op jit(solution)/shard_map/slice | solution.py:99
  235.2 5.8 %collective-permute-start.12 = (bf16[9,5,1,256]{3,2,1,0:T(2,128)(2,1)S(1)}, bf16[9,5,1,256]{3,2,1,0:T(2,128)(2,1)S(1)}, u32[]{:S(2)}, u32[]{:S(2)}) collective-permute-start(bf16[9,5,1,256]{3,2,1,0:T(2,128)(2,1)S(1)} %fusion.49), channel_id=1, source_target_pairs={{1,0},{2,1},{3,2},{5,4},{6,5},{7,6},{9,8},{10,9},{11,10},{13,12},{... | collective-permute-start | bytes 69128 | tf_op jit(solution)/shard_map/ppermute | solution.py:51
  241.1 2.3 fusion.42
  243.4 2.3 fusion.45
  245.6 2.0 pad_maximum_fusion.1
  247.6 10.2 %slice.198 = bf16[9,2,60,256]{3,2,1,0:T(8,128)(2,1)} slice(bf16[9,5,121,256]{3,2,1,0:T(8,128)(2,1)} %pad_maximum_fusion.1), slice={[0:9:1], [2:5:2], [2:121:2], [0:256:1]} | slice | bytes 1105920 | tf_op jit(solution)/shard_map/slice | solution.py:99
  257.8 10.0 %slice.196 = bf16[9,2,60,256]{3,2,1,0:T(8,128)(2,1)} slice(bf16[9,5,121,256]{3,2,1,0:T(8,128)(2,1)} %pad_maximum_fusion.1), slice={[0:9:1], [2:5:2], [1:121:2], [0:256:1]} | slice | bytes 1105920 | tf_op jit(solution)/shard_map/slice | solution.py:99
  267.9 10.3 %slice.192 = bf16[9,2,60,256]{3,2,1,0:T(8,128)(2,1)} slice(bf16[9,5,121,256]{3,2,1,0:T(8,128)(2,1)} %pad_maximum_fusion.1), slice={[0:9:1], [1:5:2], [2:121:2], [0:256:1]} | slice | bytes 1105920 | tf_op jit(solution)/shard_map/slice | solution.py:99
  278.2 5.9 %slice.190 = bf16[9,2,60,256]{3,2,1,0:T(8,128)(2,1)} slice(bf16[9,5,121,256]{3,2,1,0:T(8,128)(2,1)S(1)} %copy-done.3), slice={[0:9:1], [1:5:2], [1:121:2], [0:256:1]} | slice | bytes 1105920 | tf_op jit(solution)/shard_map/slice | solution.py:99
  284.1 5.8 %slice.184 = bf16[9,2,60,256]{3,2,1,0:T(8,128)(2,1)} slice(bf16[9,5,121,256]{3,2,1,0:T(8,128)(2,1)S(1)} %copy-done.3), slice={[0:9:1], [0:4:2], [1:121:2], [0:256:1]} | slice | bytes 1105920 | tf_op jit(solution)/shard_map/slice | solution.py:99
  (105 shorter events, 40.6 us)
Async XLA Ops:
  6.5 11.4 %copy-start.14 = (bf16[32,768]{1,0:T(8,128)(2,1)S(1)}, bf16[32,768]{1,0:T(8,128)(2,1)}, u32[]{:S(2)}) copy-start(bf16[32,768]{1,0:T(8,128)(2,1)} %param.9) | copy-start | bytes 147460
  6.5 57.4 %all-gather.3.cloned.1.call-start = ((), (), s32[]{:S(2)}) async-start(), calls=%async_computation | async-start | bytes 1327104 | tf_op jit(solution)/shard_map/all_gather | solution.py:130
  7.3 197.0 %all-gather.5.cloned.1.call-start = ((), (), s32[]{:S(2)}) async-start(), calls=%async_computation.1 | async-start | bytes 1327104 | tf_op jit(solution)/shard_map/all_gather | solution.py:132
  7.3 10.8 %collective-permute-start.4 = (bf16[32,768]{1,0:T(8,128)(2,1)}, bf16[32,768]{1,0:T(8,128)(2,1)S(1)}, u32[]{:S(2)}, u32[]{:S(2)}) collective-permute-start(bf16[32,768]{1,0:T(8,128)(2,1)} %param.9), channel_id=1, source_target_pairs={{0,4},{4,8},{8,12},{12,16},{16,20},{20,24},{24,28},{28,0},{1,5},{5... | collective-permute-start | bytes 147464 | tf_op jit(solution)/shard_map/ppermute | solution.py:19
  8.6 10.0 %collective-permute-start.5 = (bf16[32,768]{1,0:T(8,128)(2,1)}, bf16[32,768]{1,0:T(8,128)(2,1)S(1)}, u32[]{:S(2)}, u32[]{:S(2)}) collective-permute-start(bf16[32,768]{1,0:T(8,128)(2,1)} %param.9), channel_id=1, source_target_pairs={{0,28},{4,0},{8,4},{12,8},{16,12},{20,16},{24,20},{28,24},{1,29},{... | collective-permute-start | bytes 147464 | tf_op jit(solution)/shard_map/ppermute | solution.py:24
  10.9 44.2 %collective-permute-start.1 = (bf16[9,1,120,256]{3,2,1,0:T(8,128)(2,1)}, bf16[9,1,120,256]{3,2,1,0:T(8,128)(2,1)}, u32[]{:S(2)}, u32[]{:S(2)}) collective-permute-start(bf16[9,1,120,256]{3,2,1,0:T(8,128)(2,1)} %get-tuple-element.10), channel_id=1, source_target_pairs={{4,0},{8,4},{12,8},{16,12},{20,16},{24,20},{28,24},{5,1},{9,5},{13... | collective-permute-start | bytes 1658888 | tf_op jit(solution)/shard_map/ppermute | solution.py:41
  15.9 36.3 %collective-permute-start = (bf16[9,1,120,256]{3,2,1,0:T(8,128)(2,1)S(1)}, bf16[9,1,120,256]{3,2,1,0:T(8,128)(2,1)}, u32[]{:S(2)}, u32[]{:S(2)}) collective-permute-start(bf16[9,1,120,256]{3,2,1,0:T(8,128)(2,1)S(1)} %get-tuple-element.9), channel_id=1, source_target_pairs={{0,4},{4,8},{8,12},{12,16},{16,20},{20,24},{24,28},{1,5},{5,9},{9,... | collective-permute-start | bytes 1658888 | tf_op jit(solution)/shard_map/ppermute | solution.py:39
  18.1 25.9 %collective-permute-start.6 = (bf16[32,768]{1,0:T(8,128)(2,1)S(1)}, bf16[32,768]{1,0:T(8,128)(2,1)S(1)}, u32[]{:S(2)}, u32[]{:S(2)}) collective-permute-start(bf16[32,768]{1,0:T(8,128)(2,1)S(1)} %collective-permute-done.4), channel_id=1, source_target_pairs={{0,4},{4,8},{8,12},{12,16},{16,20},{20,24},{24,28},{28,0},{1,5},{5... | collective-permute-start | bytes 147464 | tf_op jit(solution)/shard_map/ppermute | solution.py:19
  18.7 25.5 %collective-permute-start.7 = (bf16[32,768]{1,0:T(8,128)(2,1)S(1)}, bf16[32,768]{1,0:T(8,128)(2,1)S(1)}, u32[]{:S(2)}, u32[]{:S(2)}) collective-permute-start(bf16[32,768]{1,0:T(8,128)(2,1)S(1)} %collective-permute-done.5), channel_id=1, source_target_pairs={{0,28},{4,0},{8,4},{12,8},{16,12},{20,16},{24,20},{28,24},{1,29},{... | collective-permute-start | bytes 147464 | tf_op jit(solution)/shard_map/ppermute | solution.py:24
  44.0 2.9 collective-permute-start.8
  44.2 3.9 %collective-permute-start.9 = (bf16[32,768]{1,0:T(8,128)(2,1)S(1)}, bf16[32,768]{1,0:T(8,128)(2,1)S(1)}, u32[]{:S(2)}, u32[]{:S(2)}) collective-permute-start(bf16[32,768]{1,0:T(8,128)(2,1)S(1)} %collective-permute-done.7), channel_id=1, source_target_pairs={{0,28},{4,0},{8,4},{12,8},{16,12},{20,16},{24,20},{28,24},{1,29},{... | collective-permute-start | bytes 147464 | tf_op jit(solution)/shard_map/ppermute | solution.py:24
  46.9 4.5 %collective-permute-start.10 = (bf16[32,768]{1,0:T(8,128)(2,1)S(1)}, bf16[32,768]{1,0:T(8,128)(2,1)S(1)}, u32[]{:S(2)}, u32[]{:S(2)}) collective-permute-start(bf16[32,768]{1,0:T(8,128)(2,1)S(1)} %collective-permute-done.8), channel_id=1, source_target_pairs={{0,4},{4,8},{8,12},{12,16},{16,20},{20,24},{24,28},{28,0},{1,5},{5... | collective-permute-start | bytes 147464 | tf_op jit(solution)/shard_map/ppermute | solution.py:19
  56.3 14.0 %collective-permute-start.2 = (bf16[9,6,1,256]{3,2,1,0:T(2,128)(2,1)S(1)}, bf16[9,6,1,256]{3,2,1,0:T(2,128)(2,1)S(1)}, u32[]{:S(2)}, u32[]{:S(2)}) collective-permute-start(bf16[9,6,1,256]{3,2,1,0:T(2,128)(2,1)S(1)} %get-tuple-element.6), channel_id=1, source_target_pairs={{0,1},{1,2},{2,3},{4,5},{5,6},{6,7},{8,9},{9,10},{10,11},{12,13},{... | collective-permute-start | bytes 82952 | tf_op jit(solution)/shard_map/ppermute | solution.py:39
  62.0 14.0 %collective-permute-start.3 = (bf16[9,6,1,256]{3,2,1,0:T(2,128)(2,1)S(1)}, bf16[9,6,1,256]{3,2,1,0:T(2,128)(2,1)S(1)}, u32[]{:S(2)}, u32[]{:S(2)}) collective-permute-start(bf16[9,6,1,256]{3,2,1,0:T(2,128)(2,1)S(1)} %get-tuple-element.5), channel_id=1, source_target_pairs={{1,0},{2,1},{3,2},{5,4},{6,5},{7,6},{9,8},{10,9},{11,10},{13,12},{... | collective-permute-start | bytes 82952 | tf_op jit(solution)/shard_map/ppermute | solution.py:41
  64.0 4.6 %copy-start = (bf16[9,4,120,256]{3,2,1,0:T(8,128)(2,1)S(1)}, bf16[9,4,120,256]{3,2,1,0:T(8,128)(2,1)}, u32[]{:S(2)}) copy-start(bf16[9,4,120,256]{3,2,1,0:T(8,128)(2,1)} %param.7) | copy-start | bytes 6635524
  64.0 4.6 %copy-start.13 = (bf16[256,2304]{1,0:T(8,128)(2,1)S(1)}, bf16[256,2304]{1,0:T(8,128)(2,1)}, u32[]{:S(2)}) copy-start(bf16[256,2304]{1,0:T(8,128)(2,1)} %all-gather.3.cloned.1.call-done) | copy-start | bytes 3538948
  101.3 1.6 copy-start.1
  104.4 1.5 slice-start.1
  106.0 1.6 copy-start.2
  110.6 85.5 %copy-start.15 = (f32[256]{0:T(256)S(1)}, f32[256]{0:T(256)}, u32[]{:S(2)}) copy-start(f32[256]{0:T(256)} %param.12) | copy-start | bytes 3076
  110.6 85.5 %copy-start.16 = (f32[256]{0:T(256)S(1)}, f32[256]{0:T(256)}, u32[]{:S(2)}) copy-start(f32[256]{0:T(256)} %param.11) | copy-start | bytes 3076
  200.6 14.2 %collective-permute-start.11 = (bf16[9,1,120,256]{3,2,1,0:T(8,128)(2,1)}, bf16[9,1,120,256]{3,2,1,0:T(8,128)(2,1)S(1)}, u32[]{:S(2)}, u32[]{:S(2)}) collective-permute-start(bf16[9,1,120,256]{3,2,1,0:T(8,128)(2,1)} %slice.226), channel_id=1, source_target_pairs={{4,0},{8,4},{12,8},{16,12},{20,16},{24,20},{28,24},{5,1},{9,5},{13... | collective-permute-start | bytes 1658888 | tf_op jit(solution)/shard_map/ppermute | solution.py:51
  235.2 5.9 %copy-start.10 = (bf16[9,2,60,256]{3,2,1,0:T(8,128)(2,1)S(1)}, bf16[9,2,60,256]{3,2,1,0:T(8,128)(2,1)}, u32[]{:S(2)}) copy-start(bf16[9,2,60,256]{3,2,1,0:T(8,128)(2,1)} %slice.194) | copy-start | bytes 1658884
  235.2 10.4 %collective-permute-start.12 = (bf16[9,5,1,256]{3,2,1,0:T(2,128)(2,1)S(1)}, bf16[9,5,1,256]{3,2,1,0:T(2,128)(2,1)S(1)}, u32[]{:S(2)}, u32[]{:S(2)}) collective-permute-start(bf16[9,5,1,256]{3,2,1,0:T(2,128)(2,1)S(1)} %fusion.49), channel_id=1, source_target_pairs={{1,0},{2,1},{3,2},{5,4},{6,5},{7,6},{9,8},{10,9},{11,10},{13,12},{... | collective-permute-start | bytes 69128 | tf_op jit(solution)/shard_map/ppermute | solution.py:51
  247.6 30.6 %copy-start.3 = (bf16[9,5,121,256]{3,2,1,0:T(8,128)(2,1)S(1)}, bf16[9,5,121,256]{3,2,1,0:T(8,128)(2,1)}, u32[]{:S(2)}) copy-start(bf16[9,5,121,256]{3,2,1,0:T(8,128)(2,1)} %pad_maximum_fusion.1) | copy-start | bytes 8363524
  290.9 3.1 copy-start.9
  290.9 4.3 %copy-start.8 = (bf16[9,2,60,256]{3,2,1,0:T(8,128)(2,1)S(1)}, bf16[9,2,60,256]{3,2,1,0:T(8,128)(2,1)}, u32[]{:S(2)}) copy-start(bf16[9,2,60,256]{3,2,1,0:T(8,128)(2,1)} %slice.190) | copy-start | bytes 1658884
  292.4 4.2 %copy-start.6 = (f32[9,2,60,256]{3,2,1,0:T(8,128)S(1)}, f32[9,2,60,256]{3,2,1,0:T(8,128)}, u32[]{:S(2)}) copy-start(f32[9,2,60,256]{3,2,1,0:T(8,128)} %fusion.46) | copy-start | bytes 3317764
  292.4 4.2 %copy-start.7 = (bf16[9,2,60,256]{3,2,1,0:T(8,128)(2,1)S(1)}, bf16[9,2,60,256]{3,2,1,0:T(8,128)(2,1)}, u32[]{:S(2)}) copy-start(bf16[9,2,60,256]{3,2,1,0:T(8,128)(2,1)} %slice.184) | copy-start | bytes 1658884
  295.2 2.6 copy-start.4
  295.2 2.6 copy-start.5
  295.2 2.6 copy-start.17
  (3 other events, 3.7 us)
Sparse Core Ops, SparseCore 0:
  9.5 53.7 all-gather.2
  65.5 39.3 all-gather.4
